TPU v7x, 32 devices: a whole 2x2x4 slice. The times are simulated.
32 devices in a mesh: seq: 16 (over z, y, x), ch: 2 (over core).
Axes of the slice: x: 2, y: 2, z: 4, core: 2. Of those that a mesh axis runs over, the one named last changes fastest.
Arguments:
- seq_values: bfloat16 [1024, 512, 512], P('ch', 'seq'), may hold values from -6 to 6
- gate_values: bfloat16 [1024, 512, 512], P('ch', 'seq'), may hold values from -6 to 6
- out_grad: bfloat16 [1024, 512, 512], P('ch', 'seq'), may hold values from -6 to 6
- factor_one: bfloat16 [512, 512], replicated, may hold values from -0.25 to 0.25
- factor_two: bfloat16 [512, 512], replicated, may hold values from -0.25 to 0.25
- twiddle: bfloat16 [512, 512], P('seq'), may hold values from 0.3984375 to 1.59375
Outputs:
- values_grad: bfloat16 [1024, 512, 512], P('ch', 'seq')
- gate_grad: bfloat16 [1024, 512, 512], P('ch', 'seq')
- factor_one_grad: float32 [512, 512], P('seq')
- factor_two_grad: float32 [512, 512], P('seq')
- twiddle_grad: float32 [512, 512], P('seq')
All inputs are finite; a program needn't handle non-finite values.
Results may differ from a plain program's by a relative error of at most 0.0064.
Values may be sent and summed in bfloat16 or wider, within the bound.
No kernel may reach another device: no remote copies, remote signals or barrier semaphores. Data moves between devices by JAX's collectives and lax.ppermute only.
A program may use at most 256 MiB of HBM per device.

v0:
```python
import jax
import jax.numpy as jnp
from jax import lax
from jax.sharding import PartitionSpec as P


def second_backward(grad_across, gathered, factor_two):
    block_grad = jnp.einsum(
        "cjr,jb->cbr", grad_across, factor_two, preferred_element_type=jnp.float32
    ).astype(jnp.bfloat16)
    second_part = jnp.einsum(
        "cjr,cbr->jb", grad_across, gathered, preferred_element_type=jnp.float32
    )
    return (block_grad, second_part)


def body(seq_values, gate_values, out_grad, factor_one, factor_two, twiddle):
    f32 = jnp.float32
    width = seq_values.shape[0] * lax.axis_size("ch")
    blocks = factor_two.shape[0]
    block_len = factor_one.shape[0]
    twiddle_f = twiddle.astype(f32)
    pre_twiddle = jnp.einsum("cbs,rs->cbr", seq_values, factor_one, preferred_element_type=f32)
    mixed_first = (pre_twiddle * twiddle_f[None]).astype(jnp.bfloat16)
    pieces = lax.all_to_all(mixed_first, "seq", split_axis=2, concat_axis=1, tiled=True)
    product = jnp.einsum("cbr,jb->cjr", pieces, factor_two, preferred_element_type=f32)
    mixed_across = product.astype(jnp.bfloat16)
    mixed = lax.all_to_all(mixed_across, "seq", split_axis=1, concat_axis=2, tiled=True)
    gate_grad = (out_grad.astype(f32) * mixed.astype(f32)).astype(jnp.bfloat16)
    mixed_grad = (gate_values.astype(f32) * out_grad.astype(f32)).astype(jnp.bfloat16)
    grad_across = lax.all_to_all(mixed_grad, "seq", split_axis=2, concat_axis=1, tiled=True)
    block_grad, second_part = second_backward(grad_across, pieces, factor_two)
    first_grad = lax.all_to_all(block_grad, "seq", split_axis=1, concat_axis=2, tiled=True)
    first_grad_f = first_grad.astype(f32)
    scaled_grad = (first_grad_f * twiddle_f[None]).astype(jnp.bfloat16)
    twiddle_part = jnp.sum(first_grad_f * pre_twiddle, axis=0)
    values_grad = jnp.einsum(
        "cbr,rs->cbs", scaled_grad, factor_one, preferred_element_type=f32
    ).astype(jnp.bfloat16)
    first_part = jnp.einsum("cbr,cbs->rs", scaled_grad, seq_values, preferred_element_type=f32)
    one_total, two_total, twiddle_total = lax.psum((first_part, second_part, twiddle_part), "ch")
    one_rows, two_rows = (
        lax.psum_scatter(one_total, "seq", scatter_dimension=0, tiled=True),
        lax.psum_scatter(two_total, "seq", scatter_dimension=0, tiled=True),
    )
    factor_one_grad = one_rows * (1.0 / (width * blocks) ** 0.5)
    factor_two_grad = two_rows * (1.0 / (width * block_len) ** 0.5)
    twiddle_grad = twiddle_total * (1.0 / width**0.5)
    return (values_grad, gate_grad, factor_one_grad, factor_two_grad, twiddle_grad)


def solution(mesh):
    return jax.shard_map(
        body,
        mesh=mesh,
        in_specs=(
            P("ch", "seq", None),
            P("ch", "seq", None),
            P("ch", "seq", None),
            P(),
            P(),
            P("seq", None),
        ),
        out_specs=(
            P("ch", "seq", None),
            P("ch", "seq", None),
            P("seq", None),
            P("seq", None),
            P("seq", None),
        ),
        check_vma=False,
    )
```

profile of v0, /device:TPU:0, one launch (start us, length us, event | category | flops | bytes accessed | tf_op | source)
XLA Modules:
  0.0 2131.9 jit_solution(16054058717922054302)
XLA Ops:
  7.2 26.2 %copy.41 = bf16[512,32,512]{0,2,1:T(8,128)(2,1)} copy(bf16[512,32,512]{2,1,0:T(8,128)(2,1)} %param.8) | data formatting | bytes 33554432 | tf_op args[2]
  33.4 26.2 %copy.40 = bf16[512,32,512]{0,2,1:T(8,128)(2,1)} copy(bf16[512,32,512]{2,1,0:T(8,128)(2,1)} %param.7) | data formatting | bytes 33554432 | tf_op args[1]
  59.6 13.3 fusion
  72.9 24.7 %copy.42 = bf16[512,32,512]{0,1,2:T(8,128)(2,1)S(1)} copy(bf16[512,32,512]{0,2,1:T(8,128)(2,1)S(1)} %fusion) | data formatting | bytes 33554432 | tf_op jit(solution)/shard_map/convert_element_type | solution.py:30
  97.6 371.5 %all_to_all.54 = bf16[512,32,512]{0,1,2:T(8,128)(2,1)S(1)} all-to-all(bf16[512,32,512]{0,1,2:T(8,128)(2,1)S(1)} %copy.42), channel_id=1, replica_groups=mesh['seq'=16,'ch'=2] {'seq'}, dimensions={2} | all-to-all | bytes 33554432 | tf_op jit(solution)/shard_map/all_to_all | solution.py:31
  469.1 11.1 copy.44
  480.2 46.3 %convert_bitcast_fusion.3 = bf16[512,512,32]{1,0,2:T(8,128)(2,1)} fusion(bf16[512,512,32]{0,2,1:T(8,128)(2,1)} %bitcast.47, bf16[512,512]{1,0:T(8,128)(2,1)S(1)} %copy-done.2), kind=kOutput, calls=%fused_computation.10 | convolution fusion | flops 8598323200 | bytes 34078720 | tf_op jit(solution)/shard_map/cjr,jb->cbr/dot_general | solution.py:8
  526.5 28.7 %copy.46 = bf16[512,512,32]{0,2,1:T(8,128)(2,1)} copy(bf16[512,512,32]{1,0,2:T(8,128)(2,1)} %convert_bitcast_fusion.3) | data formatting | bytes 33554432 | tf_op jit(solution)/shard_map/convert_element_type | solution.py:10
  555.2 5.3 all-to-all-start.1
  560.5 311.1 %all-to-all-done.1 = bf16[512,512,32]{0,2,1:T(8,128)(2,1)} async-done(((bf16[512,512,32]{0,2,1:T(8,128)(2,1)}), bf16[512,512,32]{0,2,1:T(8,128)(2,1)}, u32[]{:S(2)}, u32[]{:S(2)}) %all-to-all-start.1) | async-done | bytes 16777248 | tf_op jit(solution)/shard_map/all_to_all | solution.py:33
  871.6 9.8 convert_bitcast_fusion.1
  881.4 11.9 copy.47
  893.3 33.4 %copy.48 = f32[512,32,512]{2,0,1:T(8,128)} copy(f32[512,32,512]{0,2,1:T(8,128)} %bitcast.43) | data formatting | bytes 67108864 | tf_op jit(solution)/shard_map/convert_element_type | solution.py:34
  926.7 28.6 %multiply_reduce_fusion = (f32[32,512]{1,0:T(8,128)}, bf16[512,32,512]{2,0,1:T(8,128)(2,1)}) fusion(f32[512,32,512]{2,0,1:T(8,128)} %copy.48, f32[32,512]{1,0:T(8,128)S(1)} %convert_element_type.70, bf16[512,512]{1,0:T(8,128)(2,1)S(1)} %copy-done, bf16[512,32,512]{2,1,0:T(8,128)(2,1)} %param.6), kind=kOutput, calls=%fused_computation.6 | convolution fusion | flops 8623472640 | bytes 67764224 | tf_op jit(solution)/shard_map/cbs,rs->cbr/dot_general | solution.py:23
  955.3 28.6 %copy.50 = bf16[512,32,512]{0,1,2:T(8,128)(2,1)} copy(bf16[512,32,512]{2,0,1:T(8,128)(2,1)} %get-tuple-element.24) | data formatting | bytes 33554432 | tf_op jit(solution)/shard_map/convert_element_type | solution.py:24
  983.9 434.2 %all_to_all.55 = bf16[512,32,512]{0,1,2:T(8,128)(2,1)S(1)} all-to-all(bf16[512,32,512]{0,1,2:T(8,128)(2,1)} %copy.50), channel_id=1, replica_groups=mesh['seq'=16,'ch'=2] {'seq'}, dimensions={2} | all-to-all | bytes 33554432 | tf_op jit(solution)/shard_map/all_to_all | solution.py:25
  1418.1 11.2 copy.52
  1429.3 26.3 %copy.53 = bf16[512,512,32]{1,0,2:T(8,128)(2,1)} copy(bf16[512,512,32]{0,2,1:T(8,128)(2,1)} %bitcast.46) | data formatting | bytes 33554432 | tf_op jit(solution)/shard_map/all_to_all | solution.py:25
  1455.6 18.3 convert_bitcast_fusion.2
  1473.9 28.6 %copy.54 = bf16[512,512,32]{0,2,1:T(8,128)(2,1)} copy(bf16[512,512,32]{1,0,2:T(8,128)(2,1)} %convert_bitcast_fusion.2) | data formatting | bytes 33554432 | tf_op jit(solution)/shard_map/convert_element_type | solution.py:27
  1502.5 5.2 all-to-all-start.3
  1507.7 37.1 %fusion.15 = f32[512,512]{1,0:T(8,128)} fusion(bf16[512,32,512]{2,1,0:T(8,128)(2,1)} %param.6, f32[512,32,512]{2,0,1:T(8,128)} %copy.48, f32[32,512]{1,0:T(8,128)S(1)} %convert_element_type.70), kind=kOutput, calls=%fused_computation.21 | convolution fusion | flops 8606711808 | bytes 51445760 | tf_op jit(solution)/shard_map/cbr,cbs->rs/dot_general | solution.py:40
  1544.9 34.1 %fusion.12 = f32[512,512]{1,0:T(8,128)} fusion(bf16[512,512,32]{1,0,2:T(8,128)(2,1)} %copy.53, bf16[512,512,32]{0,2,1:T(8,128)(2,1)} %bitcast.48), kind=kOutput, calls=%fused_computation.20 | convolution fusion | flops 8589934592 | bytes 34603008 | tf_op jit(solution)/shard_map/cjr,cbr->jb/dot_general | solution.py:11
  1579.1 317.2 %reduce-scatter.3.cloned.1.call-done = f32[32,512]{1,0:T(8,128)} async-done(((f32[512,512]{1,0:T(8,128)}), f32[32,512]{1,0:T(8,128)}) %reduce-scatter.3.cloned.1.call-update) | async-done | bytes 65552 | tf_op jit(solution)/shard_map/reduce_scatter | solution.py:43
  1896.3 91.3 %reduce-scatter.5.cloned.1.call-done = f32[32,512]{1,0:T(8,128)} async-done(((f32[512,512]{1,0:T(8,128)}), f32[32,512]{1,0:T(8,128)}) %reduce-scatter.5.cloned.1.call-update) | async-done | bytes 65552 | tf_op jit(solution)/shard_map/reduce_scatter | solution.py:44
  1987.7 21.2 convolution_convert_fusion
  2008.8 18.5 copy.61
  2028.8 1.5 broadcast_multiply_fusion
  2030.3 21.1 convert_bitcast_fusion
  2051.4 25.8 %copy.55 = f32[512,32,16,32]{0,3,2,1:T(8,128)} copy(f32[512,32,16,32]{0,3,1,2:T(8,128)} %convert_bitcast_fusion) | data formatting | bytes 67108864 | tf_op jit(solution)/shard_map/convert_element_type | solution.py:29
  2077.2 19.5 fusion.1
  2096.6 28.5 %copy.62 = bf16[512,32,512]{2,1,0:T(8,128)(2,1)} copy(bf16[512,32,512]{0,2,1:T(8,128)(2,1)} %fusion.1) | data formatting | bytes 33554432
  (25 shorter events, 1.7 us)
Async XLA Ops:
  7.2 919.5 %copy-start = (bf16[512,512]{1,0:T(8,128)(2,1)S(1)}, bf16[512,512]{1,0:T(8,128)(2,1)}, u32[]{:S(2)}) copy-start(bf16[512,512]{1,0:T(8,128)(2,1)} %param.9) | copy-start | bytes 1572868
  469.1 11.1 copy-start.2
  555.2 5.3 copy-start.1
  555.2 316.4 %all-to-all-start.1 = ((bf16[512,512,32]{0,2,1:T(8,128)(2,1)}), bf16[512,512,32]{0,2,1:T(8,128)(2,1)}, u32[]{:S(2)}, u32[]{:S(2)}) async-start(bf16[512,512,32]{0,2,1:T(8,128)(2,1)} %copy.46), calls=%async_computation.1 | async-start | bytes 33554432 | tf_op jit(solution)/shard_map/all_to_all | solution.py:33
  1502.5 527.8 %all-to-all-start.3 = ((bf16[512,512,32]{0,2,1:T(8,128)(2,1)}), bf16[512,512,32]{0,2,1:T(8,128)(2,1)}, u32[]{:S(2)}, u32[]{:S(2)}) async-start(bf16[512,512,32]{0,2,1:T(8,128)(2,1)} %copy.54), calls=%async_computation.3 | async-start | bytes 33554432 | tf_op jit(solution)/shard_map/all_to_all | solution.py:28
  1507.7 388.6 %reduce-scatter.3.cloned.1.call-start = ((), (), s32[]{:S(2)}) async-start(), calls=%async_computation.6 | async-start | bytes 1114112 | tf_op jit(solution)/shard_map/reduce_scatter | solution.py:43
  1544.8 442.8 %reduce-scatter.5.cloned.1.call-start = ((), (), s32[]{:S(2)}) async-start(), calls=%async_computation.7 | async-start | bytes 1114112 | tf_op jit(solution)/shard_map/reduce_scatter | solution.py:44
  1579.0 448.3 %all-reduce.3.cloned.1.call-start = ((), (), s32[]{:S(2)}) async-start(), calls=%async_computation.8 | async-start | bytes 393216 | tf_op jit(solution)/shard_map/psum | solution.py:41
  2030.3 46.8 %slice-start = ((s8[16777216]{0:T(1024)(128)(4,1)}), s8[4194304]{0:T(1024)(128)(4,1)S(1)}, s32[]{:S(2)}) async-start(s8[16777216]{0:T(1024)(128)(4,1)} %bitcast.41), calls=%async_computation.9 | async-start | bytes 8388608
  2030.3 46.8 %slice-start.1 = ((s8[16777216]{0:T(1024)(128)(4,1)}), s8[4194304]{0:T(1024)(128)(4,1)S(1)}, s32[]{:S(2)}) async-start(s8[16777216]{0:T(1024)(128)(4,1)} %bitcast.41), calls=%async_computation.10 | async-start | bytes 8388608
  2051.4 25.8 %slice-start.2 = ((s8[16777216]{0:T(1024)(128)(4,1)}), s8[4194304]{0:T(1024)(128)(4,1)S(1)}, s32[]{:S(2)}) async-start(s8[16777216]{0:T(1024)(128)(4,1)} %bitcast.41), calls=%async_computation.11 | async-start | bytes 8388608
  2051.4 25.8 %slice-start.3 = ((s8[16777216]{0:T(1024)(128)(4,1)}), s8[4194304]{0:T(1024)(128)(4,1)S(1)}, s32[]{:S(2)}) async-start(s8[16777216]{0:T(1024)(128)(4,1)} %bitcast.41), calls=%async_computation.12 | async-start | bytes 8388608
Sparse Core Ops, SparseCore 0:
  1544.9 351.3 reduce-scatter.2
  1898.5 89.0 reduce-scatter.4
  1990.7 14.5 all-reduce.2
where the time goes:
time: 2140 us; the launch traced here: 2130 us
  blocking collectives  806 us (38%)
  waiting for transfers between devices  720 us (34%)
  local copies, waits for them, and re-layouts  330 us (15%)
  matrix products  185 us (9%)
  other arithmetic  66.7 us (3%)
    all_to_all x1, blocking collectives, body(): lax.all_to_all(mixed_first, 'seq', split_axis=2, concat_axis=1, tiled=True)  434 us
    all_to_all x1, blocking collectives, body(): lax.all_to_all(mixed_grad, 'seq', split_axis=2, concat_axis=1, tiled=True)  372 us
    reduce_scatter x1, waiting for transfers between devices, body(): lax.psum_scatter(one_total, 'seq', scatter_dimension=0, tiled=True)  317 us
    all_to_all x1, waiting for transfers between devices, body(): lax.all_to_all(block_grad, 'seq', split_axis=1, concat_axis=2, tiled=True)  311 us
    unnamed x18, local copies, waits for them, and re-layouts  99.4 us
    reduce_scatter x1, waiting for transfers between devices, body(): lax.psum_scatter(two_total, 'seq', scatter_dimension=0, tiled=True)  91.3 us
    dot_general x1, matrix products, second_backward(): jnp.einsum('cjr,jb->cbr', grad_across, factor_two, preferred_element_type...  46.3 us
    convert_element_type x2, local copies, waits for them, and re-layouts, body(): first_grad_f = first_grad.astype(f32)  45.2 us
  transfers between devices with their start and end apart: 5, of which 3 were waited for; matrix products, arithmetic and copies ran while one was open for 5% of the time, Pallas kernels for 0%

commit v1 on v0

v1 whole, which is shorter than its diff:
```python
import math

import jax
import jax.numpy as jnp
from jax import lax
from jax.experimental import pallas as pl
from jax.experimental.pallas import tpu as pltpu
from jax.sharding import PartitionSpec as P

f32 = jnp.float32
bf16 = jnp.bfloat16


def dot(a, b, dims):
    return lax.dot_general(a, b, (dims, ((), ())), preferred_element_type=f32)


def first_kernel(x_ref, f1_ref, tw_ref, out_ref):
    p, n, b, s = x_ref.shape
    pre = dot(x_ref[...].reshape(p * n * b, s), f1_ref[...], ((1,), (1,)))
    out = pre.reshape(p * n, b, -1) * tw_ref[...].astype(f32)[None]
    out_ref[...] = out.astype(bf16).reshape(p, n, b, s)


def product_kernel(g_ref, o_ref, out_ref):
    out_ref[...] = (g_ref[...].astype(f32) * o_ref[...].astype(f32)).astype(bf16)


def mix_grad_kernel(g_ref, f2t_ref, out_ref):
    a, n, b, s = g_ref.shape
    for i in range(n):
        got = dot(f2t_ref[...], g_ref[:, i].reshape(a * b, s), ((1,), (0,)))
        out_ref[:, i] = got.astype(bf16).reshape(a, b, s)


def at_start():
    return (pl.program_id(0) == 0) & (pl.program_id(1) == 0)


def mix_kernel(v_ref, g_ref, f2_ref, out_ref, sum_ref):
    a, n, b, s = v_ref.shape

    @pl.when(at_start())
    def _():
        sum_ref[...] = jnp.zeros(sum_ref.shape, f32)

    for i in range(n):
        vals = v_ref[:, i].reshape(a * b, s)
        out_ref[:, i] = dot(f2_ref[...], vals, ((1,), (0,))).astype(bf16).reshape(a, b, s)
        sum_ref[...] += dot(g_ref[:, i].reshape(a * b, s), vals, ((1,), (1,)))


def last_kernel(d_ref, x_ref, f1_ref, tw_ref, out_ref, one_ref, tw_sum_ref):
    p, n, b, s = x_ref.shape

    @pl.when(at_start())
    def _():
        one_ref[...] = jnp.zeros(one_ref.shape, f32)
        tw_sum_ref[...] = jnp.zeros(tw_sum_ref.shape, f32)

    x = x_ref[...].reshape(p * n * b, s)
    pre = dot(x, f1_ref[...], ((1,), (1,))).reshape(p * n, b, -1)
    grad = d_ref[...].astype(f32).reshape(p * n, b, -1)
    tw_sum_ref[...] += jnp.sum(grad * pre, axis=0)
    scaled = (grad * tw_ref[...].astype(f32)[None]).astype(bf16).reshape(p * n * b, -1)
    out_ref[...] = dot(scaled, f1_ref[...], ((1,), (0,))).astype(bf16).reshape(p, n, b, s)
    one_ref[...] += dot(scaled, x, ((0,), (0,)))


def stage(name, kernel, unit, peers, count, reads, small, write, sums=()):
    size, _, b, s = reads[0][0].shape
    peers = math.gcd(size, peers)

    def part(first):
        return pl.BlockSpec((peers, unit, b, s), lambda p, i: (p, first // unit + i, 0, 0))

    def whole(shape):
        return pl.BlockSpec(shape, lambda p, i: (0,) * len(shape))

    into, slots, first = write
    operands = [v for v, _ in reads] + list(small)
    specs = [part(at) for _, at in reads] + [whole(v.shape) for v in small]
    fixed = len(operands)
    alias = {}
    call = kernel
    if into is not None:
        alias = {fixed: 0}
        operands.append(into)
        specs.append(pl.BlockSpec(memory_space=pl.ANY))

        def call(*refs):
            kernel(*refs[:fixed], *refs[fixed + 1 :])

    out = pl.pallas_call(
        call,
        grid=(size // peers, count // unit),
        in_specs=specs,
        out_specs=[part(first)] + [whole(v) for v in sums],
        out_shape=[jax.ShapeDtypeStruct((size, slots, b, s), bf16)]
        + [jax.ShapeDtypeStruct(v, f32) for v in sums],
        input_output_aliases=alias,
        name=name,
    )(*operands)
    return out if sums else out[0]


def halve(parts, bit):
    size = lax.axis_size("seq")
    axis = parts.ndim - 3
    own = (lax.axis_index("seq") >> bit) & 1
    keep = lax.dynamic_index_in_dim(parts, own, axis, keepdims=False)
    send = lax.dynamic_index_in_dim(parts, 1 - own, axis, keepdims=False)
    pairs = [(i, i ^ (1 << bit)) for i in range(size)]
    return keep + lax.ppermute(send, "seq", pairs)


def scatter_sum(total, beside=None):
    size = lax.axis_size("seq")
    bits = size.bit_length() - 1
    rows = total.shape[0] // size
    parts = total.reshape((2,) * bits + (rows, total.shape[1]))
    for bit in range(bits):
        parts = halve(parts, bit)
        if bit == 0 and beside is not None:
            parts, beside = lax.optimization_barrier((parts, beside))
    return parts, beside


def channel_sum(value):
    size = lax.axis_size("ch")
    step = 1
    while step < size:
        value = value + lax.ppermute(value, "ch", [(i, i ^ step) for i in range(size)])
        step *= 2
    return value


def body(x, gate, og, f1, f2, tw):
    size = lax.axis_size("seq")
    own_width, b, s = x.shape
    width = own_width * lax.axis_size("ch")
    blocks = f2.shape[0]
    slots = own_width // size
    bounds = [0, max(1, slots // 8), slots // 2, slots]
    unit = math.gcd(*bounds, 4)
    counts = [hi - lo for lo, hi in zip(bounds, bounds[1:])]
    by_peer = lambda v: v.reshape(size, slots, b, s)
    x, gate, og = by_peer(x), by_peer(gate), by_peer(og)
    f2t = f2.T
    got = {}
    two_parts = []

    def make(kind, k, write):
        count, at = counts[k], bounds[k]
        if kind == "A":
            return stage("grad", product_kernel, unit, 8, count, [(gate, at), (og, at)], [], write)
        if kind == "B":
            return stage("first", first_kernel, unit, 4, count, [(x, at)], [f1, tw], write)
        if kind == "D":
            return stage("mix_grad", mix_grad_kernel, unit, size, count, [got["A", k]], [f2t], write)
        out, part = stage(
            "mix", mix_kernel, unit, size, count, [got["B", k], got["A", k]], [f2], write, [f2.shape]
        )
        two_parts.append(part)
        return out

    token = None
    two_rows = None
    plan = [
        [("A", 0)],
        [("B", 0), ("B", 1), ("A", 1), ("A", 2)],
        [("D", 0), ("B", 2)],
        [("D", 1), ("D", 2), ("C", 0), ("C", 1)],
        [("C", 2)],
    ]
    for piece in plan:
        total = sum(counts[k] for _, k in piece)
        buffer, first, places = None, 0, []
        for kind, k in piece:
            buffer = make(kind, k, (buffer, total, first))
            places.append((kind, k, first))
            first += counts[k]
        if len(two_parts) == len(counts) and two_rows is None:
            two_rows, _ = scatter_sum(sum(two_parts[1:], two_parts[0]))
            buffer, token, two_rows = lax.optimization_barrier((buffer, token, two_rows))
        elif token is not None:
            buffer, token = lax.optimization_barrier((buffer, token))
        token = lax.all_to_all(
            buffer.reshape(-1, b, s), "seq", split_axis=0, concat_axis=0, tiled=True
        )
        here = token.reshape(size, total, b, s)
        for kind, k, first in places:
            got[kind, k] = (here, first)

    values_grad = gate_grad = None
    one_parts, tw_parts = [], []
    for k, (at, count) in enumerate(zip(bounds, counts)):
        values_grad, one, tw_part = stage(
            "last", last_kernel, unit, 4, count, [got["D", k], (x, at)], [f1, tw],
            (values_grad, slots, at), [f1.shape, tw.shape],
        )
        one_parts.append(one)
        tw_parts.append(tw_part)
    for k in (0, 1):
        gate_grad = stage(
            "gate", product_kernel, unit, 8, counts[k], [got["C", k], (og, bounds[k])], [],
            (gate_grad, slots, bounds[k]),
        )
    one_rows, gate_grad = scatter_sum(sum(one_parts[1:], one_parts[0]), gate_grad)
    tw_rows = sum(tw_parts[1:], tw_parts[0])
    one_rows, two_rows, tw_rows = channel_sum(jnp.stack([one_rows, two_rows, tw_rows]))
    gate_grad = stage(
        "gate", product_kernel, unit, 8, counts[2], [got["C", 2], (og, bounds[2])], [],
        (gate_grad, slots, bounds[2]),
    )
    return (
        values_grad.reshape(own_width, b, s),
        gate_grad.reshape(own_width, b, s),
        one_rows * (1.0 / (width * blocks) ** 0.5),
        two_rows * (1.0 / (width * s) ** 0.5),
        tw_rows * (1.0 / width**0.5),
    )


def solution(mesh):
    return jax.shard_map(
        body,
        mesh=mesh,
        in_specs=(
            P("ch", "seq", None),
            P("ch", "seq", None),
            P("ch", "seq", None),
            P(),
            P(),
            P("seq", None),
        ),
        out_specs=(
            P("ch", "seq", None),
            P("ch", "seq", None),
            P("seq", None),
            P("seq", None),
            P("seq", None),
        ),
        check_vma=False,
    )
```

time: 2140 us -> 1560 us (0.73)
  blocking collectives: 806 us -> 0 us
  waiting for transfers between devices: 720 us -> 1120 us
  local copies, waits for them, and re-layouts: 330 us -> 2.74 us
  starting transfers between devices: 10.6 us -> 252 us
  matrix products: 185 us -> 0 us
  Pallas kernels: 0 us -> 180 us
  other arithmetic: 66.7 us -> 4.18 us
    all_to_all x2 -> x0, blocking collectives: 806 us -> none  [the longest x1 434 us: body(): lax.all_to_all(mixed_first, 'seq', split_axis=2, concat_axis=1, tiled=True)]
    ppermute x0 -> x9, waiting for transfers between devices: none -> 548 us  [the longest x8 546 us: halve(): return keep + lax.ppermute(send, 'seq', pairs)]
    reduce_scatter x2 -> x0, waiting for transfers between devices: 409 us -> none  [the longest x1 317 us: body(): lax.psum_scatter(one_total, 'seq', scatter_dimension=0, tiled=True)]
    all_to_all x2 -> x5, waiting for transfers between devices: 311 us -> 574 us  [body(): lax.all_to_all(buffer.reshape(-1, b, s), 'seq', split_axis=0, concat_axis...]
    all_to_all x2 -> x5, starting transfers between devices: 10.4 us -> 197 us  [body(): lax.all_to_all(buffer.reshape(-1, b, s), 'seq', split_axis=0, concat_axis...]
    dot_general x6 -> x0, matrix products: 185 us -> none  [the longest x1 46.3 us: second_backward(): jnp.einsum('cjr,jb->cbr', grad_across, factor_two, preferred_element_type...]
    convert_element_type x7 -> x0, local copies, waits for them, and re-layouts: 182 us -> none  [the longest x2 45.2 us: body(): first_grad_f = first_grad.astype(f32)]
    pallas_call x0 -> x18, Pallas kernels: none -> 180 us  [stage(): pl.pallas_call(call, grid=(size // peers, count // unit), in_specs=specs,...]
  transfers between devices with their start and end apart: 5 -> 14, of which waited for: 3 -> 11; matrix products, arithmetic and copies ran while one was open for 5% -> 0% of each run, Pallas kernels for 0% -> 11%
where the time goes in v1:
time: 1560 us
  waiting for transfers between devices  1120 us (72%)
  starting transfers between devices  252 us (16%)
  Pallas kernels  180 us (12%)
    all_to_all x5, waiting for transfers between devices, body(): lax.all_to_all(buffer.reshape(-1, b, s), 'seq', split_axis=0, concat_axis...  574 us
    ppermute x8, waiting for transfers between devices, halve(): return keep + lax.ppermute(send, 'seq', pairs)  546 us
    all_to_all x5, starting transfers between devices, body(): lax.all_to_all(buffer.reshape(-1, b, s), 'seq', split_axis=0, concat_axis...  197 us
    pallas_call x18, Pallas kernels, stage(): pl.pallas_call(call, grid=(size // peers, count // unit), in_specs=specs,...  180 us
    ppermute x8, starting transfers between devices, halve(): return keep + lax.ppermute(send, 'seq', pairs)  55.1 us
  transfers between devices with their start and end apart: 14, of which 11 were waited for; matrix products, arithmetic and copies ran while one was open for 0% of the time, Pallas kernels for 11%

profile of v1, /device:TPU:0, one launch (start us, length us, event | category | flops | bytes accessed | tf_op | source)
XLA Modules:
  0.0 1561.3 jit_solution(5507622746345448340)
XLA Ops:
  4.0 8.3 all-to-all-start
  12.4 4.9 first.3.refs_3_
  17.3 11.8 first.4.refs_2_
  29.1 8.7 grad.3.refs_2_
  37.8 11.3 grad.4
  49.1 6.3 all-to-all-done
  56.7 10.0 all-to-all-start.1
  72.1 15.3 first.5
  87.4 412.4 %all-to-all-done.1 = bf16[704,32,512]{2,1,0:T(8,128)(2,1)} async-done(((bf16[704,32,512]{2,1,0:T(8,128)(2,1)}), bf16[704,32,512]{2,1,0:T(8,128)(2,1)}, u32[]{:S(2)}, u32[]{:S(2)}) %all-to-all-start.1) | async-done | bytes 23068704 | tf_op jit(solution)/shard_map/all_to_all | solution.py:188
  499.8 98.9 %all-to-all-start.2 = ((bf16[320,32,512]{2,1,0:T(8,128)(2,1)}), bf16[320,32,512]{2,1,0:T(8,128)(2,1)}, u32[]{:S(2)}, u32[]{:S(2)}) async-start(bf16[320,32,512]{2,1,0:T(8,128)(2,1)} %bitcast.83), calls=%async_computation.2 | async-start | bytes 20971520 | tf_op jit(solution)/shard_map/all_to_all | solution.py:188
  598.8 8.1 mix_grad.3.refs_2_
  606.9 9.4 mix_grad.4.refs_3_
  616.3 6.3 mix.3
  622.6 11.7 mix.4
  634.4 154.9 %all-to-all-done.2 = bf16[320,32,512]{2,1,0:T(8,128)(2,1)} async-done(((bf16[320,32,512]{2,1,0:T(8,128)(2,1)}), bf16[320,32,512]{2,1,0:T(8,128)(2,1)}, u32[]{:S(2)}, u32[]{:S(2)}) %all-to-all-start.2) | async-done | bytes 10485792 | tf_op jit(solution)/shard_map/all_to_all | solution.py:188
  789.3 49.0 %all-to-all-start.3 = ((bf16[704,32,512]{2,1,0:T(8,128)(2,1)}), bf16[704,32,512]{2,1,0:T(8,128)(2,1)}, u32[]{:S(2)}, u32[]{:S(2)}) async-start(bf16[704,32,512]{2,1,0:T(8,128)(2,1)} %bitcast.77), calls=%async_computation.3 | async-start | bytes 46137344 | tf_op jit(solution)/shard_map/all_to_all | solution.py:188
  838.3 14.4 mix.5
  856.5 79.9 %collective-permute-done = f32[2,2,2,32,512]{4,3,1,0,2:T(8,128)S(1)} collective-permute-done((f32[2,2,2,32,512]{4,3,1,0,2:T(8,128)S(1)}, f32[2,2,2,32,512]{4,3,1,0,2:T(8,128)S(1)}, u32[]{:S(2)}, u32[]{:S(2)}) %collective-permute-start) | collective-permute-done | bytes 524320 | tf_op jit(solution)/shard_map/ppermute | solution.py:114
  936.6 31.9 %collective-permute-done.1 = f32[2,2,32,512]{3,2,1,0:T(8,128)S(1)} collective-permute-done((f32[2,2,32,512]{3,2,1,0:T(8,128)S(1)}, f32[2,2,32,512]{3,2,1,0:T(8,128)S(1)}, u32[]{:S(2)}, u32[]{:S(2)}) %collective-permute-start.1) | collective-permute-done | bytes 262176 | tf_op jit(solution)/shard_map/ppermute | solution.py:114
  968.6 242.2 %collective-permute-done.2 = f32[2,32,512]{2,1,0:T(8,128)S(1)} collective-permute-done((f32[2,32,512]{2,1,0:T(8,128)S(1)}, f32[2,32,512]{2,1,0:T(8,128)S(1)}, u32[]{:S(2)}, u32[]{:S(2)}) %collective-permute-start.2) | collective-permute-done | bytes 131104 | tf_op jit(solution)/shard_map/ppermute | solution.py:114
  1214.4 121.2 %collective-permute-done.3 = f32[32,512]{1,0:T(8,128)S(1)} collective-permute-done((f32[32,512]{1,0:T(8,128)S(1)}, f32[32,512]{1,0:T(8,128)S(1)}, u32[]{:S(2)}, u32[]{:S(2)}) %collective-permute-start.3) | collective-permute-done | bytes 65568 | tf_op jit(solution)/shard_map/ppermute | solution.py:114
  1335.7 30.6 %all-to-all-start.4 = ((bf16[256,32,512]{2,1,0:T(8,128)(2,1)}), bf16[256,32,512]{2,1,0:T(8,128)(2,1)}, u32[]{:S(2)}, u32[]{:S(2)}) async-start(bf16[256,32,512]{2,1,0:T(8,128)(2,1)} %bitcast.91), calls=%async_computation.4 | async-start | bytes 16777216 | tf_op jit(solution)/shard_map/all_to_all | solution.py:188
  1366.3 7.3 last.3
  1373.6 17.3 %last.4 = (bf16[16,32,32,512]{3,2,1,0:T(8,128)(2,1)}, f32[512,512]{1,0:T(8,128)}, f32[32,512]{1,0:T(8,128)}) custom-call(bf16[16,44,32,512]{3,2,1,0:T(8,128)(2,1)} %bitcast.10.refs_0_.g_ref, bf16[16,32,32,512]{3,2,1,0:T(8,128)(2,1)} %bitcast.69, bf16[512,512]{1,0:T(8,128)(2,1)} %refs_2_.11, ...), custom_call_target="tpu_custom_call", output_to_operand_aliasing={{0}: (4, {})} | custom-call | tf_op jit(solution)/shard_map/last/pallas_call | solution.py:94
  1390.9 22.4 %last.5 = (bf16[16,32,32,512]{3,2,1,0:T(8,128)(2,1)}, f32[512,512]{1,0:T(8,128)}, f32[32,512]{1,0:T(8,128)}) custom-call(bf16[16,44,32,512]{3,2,1,0:T(8,128)(2,1)} %bitcast.10.refs_0_.g_ref, bf16[16,32,32,512]{3,2,1,0:T(8,128)(2,1)} %bitcast.70, bf16[512,512]{1,0:T(8,128)(2,1)} %refs_2_.11, ...), custom_call_target="tpu_custom_call", output_to_operand_aliasing={{0}: (4, {})} | custom-call | tf_op jit(solution)/shard_map/last/pallas_call | solution.py:94
  1420.2 8.7 gate.4.refs_2_
  1429.1 42.5 %collective-permute-start.5 = (f32[2,2,32,512]{3,2,0,1:T(8,128)S(1)}, f32[2,2,32,512]{3,2,0,1:T(8,128)S(1)}, u32[]{:S(2)}, u32[]{:S(2)}) collective-permute-start(f32[2,2,32,512]{3,2,0,1:T(8,128)S(1)} %bitcast.98), channel_id=1, source_target_pairs={{0,4},{2,6},{4,0},{6,2},{8,12},{10,14},{12,8},{14,10},{16,20},{18,... | collective-permute-start | bytes 786440 | tf_op jit(solution)/shard_map/ppermute | solution.py:114
  1471.6 7.6 collective-permute-done.5
  1479.3 21.0 %collective-permute-done.6 = f32[2,32,512]{2,1,0:T(8,128)S(1)} collective-permute-done((f32[2,32,512]{2,1,0:T(8,128)S(1)}, f32[2,32,512]{2,1,0:T(8,128)S(1)}, u32[]{:S(2)}, u32[]{:S(2)}) %collective-permute-start.6) | collective-permute-done | bytes 131104 | tf_op jit(solution)/shard_map/ppermute | solution.py:114
  1500.4 4.9 collective-permute-start.7
  1505.4 42.4 %collective-permute-done.7 = f32[32,512]{1,0:T(8,128)S(1)} collective-permute-done((f32[32,512]{1,0:T(8,128)S(1)}, f32[32,512]{1,0:T(8,128)S(1)}, u32[]{:S(2)}, u32[]{:S(2)}) %collective-permute-start.7) | collective-permute-done | bytes 65568 | tf_op jit(solution)/shard_map/ppermute | solution.py:114
  1550.0 11.3 gate.5
  (57 shorter events, 27.1 us)
Async XLA Ops:
  4.0 51.4 %all-to-all-start = ((bf16[64,32,512]{2,1,0:T(8,128)(2,1)}), bf16[64,32,512]{2,1,0:T(8,128)(2,1)S(1)}, u32[]{:S(2)}, u32[]{:S(2)}) async-start(bf16[64,32,512]{2,1,0:T(8,128)(2,1)} %bitcast.90), calls=%async_computation | async-start | bytes 4194304 | tf_op jit(solution)/shard_map/all_to_all | solution.py:188
  55.4 1.3 copy-start
  55.4 11.4 copy-start.1
  56.7 443.1 %all-to-all-start.1 = ((bf16[704,32,512]{2,1,0:T(8,128)(2,1)}), bf16[704,32,512]{2,1,0:T(8,128)(2,1)}, u32[]{:S(2)}, u32[]{:S(2)}) async-start(bf16[704,32,512]{2,1,0:T(8,128)(2,1)} %bitcast.78), calls=%async_computation.1 | async-start | bytes 46137344 | tf_op jit(solution)/shard_map/all_to_all | solution.py:188
  499.8 289.5 %all-to-all-start.2 = ((bf16[320,32,512]{2,1,0:T(8,128)(2,1)}), bf16[320,32,512]{2,1,0:T(8,128)(2,1)}, u32[]{:S(2)}, u32[]{:S(2)}) async-start(bf16[320,32,512]{2,1,0:T(8,128)(2,1)} %bitcast.83), calls=%async_computation.2 | async-start | bytes 20971520 | tf_op jit(solution)/shard_map/all_to_all | solution.py:188
  789.3 546.3 %all-to-all-start.3 = ((bf16[704,32,512]{2,1,0:T(8,128)(2,1)}), bf16[704,32,512]{2,1,0:T(8,128)(2,1)}, u32[]{:S(2)}, u32[]{:S(2)}) async-start(bf16[704,32,512]{2,1,0:T(8,128)(2,1)} %bitcast.77), calls=%async_computation.3 | async-start | bytes 46137344 | tf_op jit(solution)/shard_map/all_to_all | solution.py:188
  838.3 14.4 copy-start.2
  838.3 14.4 copy-start.3
  854.5 81.9 %collective-permute-start = (f32[2,2,2,32,512]{4,3,1,0,2:T(8,128)S(1)}, f32[2,2,2,32,512]{4,3,1,0,2:T(8,128)S(1)}, u32[]{:S(2)}, u32[]{:S(2)}) collective-permute-start(f32[2,2,2,32,512]{4,3,1,0,2:T(8,128)S(1)} %bitcast.97), channel_id=1, source_target_pairs={{0,2},{2,0},{4,6},{6,4},{8,10},{10,8},{12,14},{14,12},{16,18},{18,... | collective-permute-start | bytes 1572872 | tf_op jit(solution)/shard_map/ppermute | solution.py:114
  936.5 31.9 %collective-permute-start.1 = (f32[2,2,32,512]{3,2,1,0:T(8,128)S(1)}, f32[2,2,32,512]{3,2,1,0:T(8,128)S(1)}, u32[]{:S(2)}, u32[]{:S(2)}) collective-permute-start(f32[2,2,32,512]{3,2,1,0:T(8,128)S(1)} %dynamic-slice_bitcast_fusion.1), channel_id=1, source_target_pairs={{0,4},{2,6},{4,0},{6,2},{8,12},{10,14},{12,8},{14,10},{16,20},{18,... | collective-permute-start | bytes 786440 | tf_op jit(solution)/shard_map/ppermute | solution.py:114
  968.5 242.3 %collective-permute-start.2 = (f32[2,32,512]{2,1,0:T(8,128)S(1)}, f32[2,32,512]{2,1,0:T(8,128)S(1)}, u32[]{:S(2)}, u32[]{:S(2)}) collective-permute-start(f32[2,32,512]{2,1,0:T(8,128)S(1)} %dynamic-slice_bitcast_fusion.3), channel_id=1, source_target_pairs={{0,8},{2,10},{4,12},{6,14},{8,0},{10,2},{12,4},{14,6},{16,24},{18,... | collective-permute-start | bytes 393224 | tf_op jit(solution)/shard_map/ppermute | solution.py:114
  1210.9 124.8 %collective-permute-start.3 = (f32[32,512]{1,0:T(8,128)S(1)}, f32[32,512]{1,0:T(8,128)S(1)}, u32[]{:S(2)}, u32[]{:S(2)}) collective-permute-start(f32[32,512]{1,0:T(8,128)S(1)} %dynamic-slice_bitcast_fusion.5), channel_id=1, source_target_pairs={{0,16},{2,18},{4,20},{6,22},{8,24},{10,26},{12,28},{14,30},{16,0},... | collective-permute-start | bytes 196616 | tf_op jit(solution)/shard_map/ppermute | solution.py:114
  1335.7 214.3 %all-to-all-start.4 = ((bf16[256,32,512]{2,1,0:T(8,128)(2,1)}), bf16[256,32,512]{2,1,0:T(8,128)(2,1)}, u32[]{:S(2)}, u32[]{:S(2)}) async-start(bf16[256,32,512]{2,1,0:T(8,128)(2,1)} %bitcast.91), calls=%async_computation.4 | async-start | bytes 16777216 | tf_op jit(solution)/shard_map/all_to_all | solution.py:188
  1390.9 22.4 %copy-start.4 = (f32[512,512]{1,0:T(8,128)S(1)}, f32[512,512]{1,0:T(8,128)}, u32[]{:S(2)}) copy-start(f32[512,512]{1,0:T(8,128)} %get-tuple-element.40) | copy-start | bytes 3145732
  1390.9 22.4 %copy-start.5 = (f32[512,512]{1,0:T(8,128)S(1)}, f32[512,512]{1,0:T(8,128)}, u32[]{:S(2)}) copy-start(f32[512,512]{1,0:T(8,128)} %get-tuple-element.41) | copy-start | bytes 3145732
  1414.9 14.1 collective-permute-start.4
  1420.2 85.2 %copy-start.6 = (f32[32,512]{1,0:T(8,128)S(1)}, f32[32,512]{1,0:T(8,128)}, u32[]{:S(2)}) copy-start(f32[32,512]{1,0:T(8,128)} %get-tuple-element.46) | copy-start | bytes 196612
  1420.2 85.2 %copy-start.7 = (f32[32,512]{1,0:T(8,128)S(1)}, f32[32,512]{1,0:T(8,128)}, u32[]{:S(2)}) copy-start(f32[32,512]{1,0:T(8,128)} %get-tuple-element.47) | copy-start | bytes 196612
  1420.2 85.2 %copy-start.8 = (f32[32,512]{1,0:T(8,128)S(1)}, f32[32,512]{1,0:T(8,128)}, u32[]{:S(2)}) copy-start(f32[32,512]{1,0:T(8,128)} %get-tuple-element.48) | copy-start | bytes 196612
  1429.1 50.1 %collective-permute-start.5 = (f32[2,2,32,512]{3,2,0,1:T(8,128)S(1)}, f32[2,2,32,512]{3,2,0,1:T(8,128)S(1)}, u32[]{:S(2)}, u32[]{:S(2)}) collective-permute-start(f32[2,2,32,512]{3,2,0,1:T(8,128)S(1)} %bitcast.98), channel_id=1, source_target_pairs={{0,4},{2,6},{4,0},{6,2},{8,12},{10,14},{12,8},{14,10},{16,20},{18,... | collective-permute-start | bytes 786440 | tf_op jit(solution)/shard_map/ppermute | solution.py:114
  1479.3 21.1 %collective-permute-start.6 = (f32[2,32,512]{2,1,0:T(8,128)S(1)}, f32[2,32,512]{2,1,0:T(8,128)S(1)}, u32[]{:S(2)}, u32[]{:S(2)}) collective-permute-start(f32[2,32,512]{2,1,0:T(8,128)S(1)} %dynamic-slice_bitcast_fusion.2), channel_id=1, source_target_pairs={{0,8},{2,10},{4,12},{6,14},{8,0},{10,2},{12,4},{14,6},{16,24},{18,... | collective-permute-start | bytes 393224 | tf_op jit(solution)/shard_map/ppermute | solution.py:114
  1500.4 47.3 %collective-permute-start.7 = (f32[32,512]{1,0:T(8,128)S(1)}, f32[32,512]{1,0:T(8,128)S(1)}, u32[]{:S(2)}, u32[]{:S(2)}) collective-permute-start(f32[32,512]{1,0:T(8,128)S(1)} %dynamic-slice_bitcast_fusion.4), channel_id=1, source_target_pairs={{0,16},{2,18},{4,20},{6,22},{8,24},{10,26},{12,28},{14,30},{16,0},... | collective-permute-start | bytes 196616 | tf_op jit(solution)/shard_map/ppermute | solution.py:114
  1547.8 1.5 collective-permute-start.8

commit v2 on v0

v2 whole, which is shorter than its diff:
```python
import math

import jax
import jax.numpy as jnp
from jax import lax
from jax.experimental import pallas as pl
from jax.experimental.pallas import tpu as pltpu
from jax.sharding import PartitionSpec as P


f32 = jnp.float32
bf16 = jnp.bfloat16
LINE = 4
CHUNKS = 2


def dot(a, b, dims):
    return lax.dot_general(a, b, (dims, ((), ())), preferred_element_type=f32)


def first_kernel(x_ref, f1_ref, tw_ref, out_ref):
    p, n, b, s = x_ref.shape
    pre = dot(x_ref[...].reshape(p * n * b, s), f1_ref[...], ((1,), (1,)))
    out = pre.reshape(p * n, b, -1) * tw_ref[...].astype(f32)[None]
    out_ref[...] = out.astype(bf16).reshape(p, n, b, s)


def product_kernel(g_ref, o_ref, out_ref):
    out_ref[...] = (g_ref[...].astype(f32) * o_ref[...].astype(f32)).astype(bf16)


def at_start():
    return (pl.program_id(0) == 0) & (pl.program_id(1) == 0)


def rows_of(refs, i):
    return jnp.concatenate([r[:, i].reshape(-1, r.shape[-1]) for r in refs], axis=0)


def write_rows(refs, i, value):
    step = value.shape[0] // len(refs)
    for k, r in enumerate(refs):
        r[:, i] = value[k * step : (k + 1) * step].reshape(r.shape[0], *r.shape[2:])


def mix_grad_kernel(*refs):
    grads, f2t_ref, outs = refs[:LINE], refs[LINE], refs[LINE + 1 :]
    for i in range(grads[0].shape[1]):
        write_rows(outs, i, dot(f2t_ref[...], rows_of(grads, i), ((1,), (0,))).astype(bf16))


def mix_kernel(*refs):
    vals, grads, f2_ref = refs[:LINE], refs[LINE : 2 * LINE], refs[2 * LINE]
    outs, sum_ref = refs[2 * LINE + 1 : -1], refs[-1]

    @pl.when(pl.program_id(0) == 0)
    def _():
        sum_ref[...] = jnp.zeros(sum_ref.shape, f32)

    for i in range(vals[0].shape[1]):
        v = rows_of(vals, i)
        write_rows(outs, i, dot(f2_ref[...], v, ((1,), (0,))).astype(bf16))
        sum_ref[...] += dot(rows_of(grads, i), v, ((1,), (1,)))


def last_kernel(d_ref, x_ref, f1_ref, tw_ref, out_ref, one_ref, tw_sum_ref):
    p, n, b, s = x_ref.shape

    @pl.when(at_start())
    def _():
        one_ref[...] = jnp.zeros(one_ref.shape, f32)
        tw_sum_ref[...] = jnp.zeros(tw_sum_ref.shape, f32)

    x = x_ref[...].reshape(p * n * b, s)
    pre = dot(x, f1_ref[...], ((1,), (1,))).reshape(p * n, b, -1)
    grad = d_ref[...].astype(f32).reshape(p * n, b, -1)
    tw_sum_ref[...] += jnp.sum(grad * pre, axis=0)
    scaled = (grad * tw_ref[...].astype(f32)[None]).astype(bf16).reshape(p * n * b, -1)
    out_ref[...] = dot(scaled, f1_ref[...], ((1,), (0,))).astype(bf16).reshape(p, n, b, s)
    one_ref[...] += dot(scaled, x, ((0,), (0,)))


def mid_stage(kernel, slabs, factor, sums=()):
    g, count, b, s = slabs[0].shape
    unit = math.gcd(count, 4)
    part = pl.BlockSpec((g, unit, b, s), lambda i: (0, i, 0, 0))
    whole = lambda shape: pl.BlockSpec(shape, lambda i: (0, 0))
    out = pl.pallas_call(
        kernel,
        grid=(count // unit,),
        in_specs=[part] * len(slabs) + [whole(factor.shape)],
        out_specs=[part] * LINE + [whole(v) for v in sums],
        out_shape=[jax.ShapeDtypeStruct(slabs[0].shape, bf16)] * LINE
        + [jax.ShapeDtypeStruct(v, f32) for v in sums],
    )(*slabs, factor)
    return list(out[:LINE]), list(out[LINE:])


def stage(kernel, most, line, lo, slab, count, wide, small, into=False, sums=()):
    size, slots, b, s = wide[0].shape
    g = size // LINE
    unit = math.gcd(count, lo, most)
    at = lambda one, i, z: (z[0], lo // unit + i, 0, 0)
    own = lambda one, i, z: (0, i, 0, 0)
    block = (g, unit, b, s)
    whole = lambda shape: pl.BlockSpec(shape, lambda one, i, z: (0,) * len(shape))
    operands = ([] if slab is None else [slab]) + list(wide) + list(small)
    specs = [] if slab is None else [pl.BlockSpec(block, own)]
    specs += [pl.BlockSpec(block, at) for _ in wide] + [whole(v.shape) for v in small]
    fixed = len(operands)
    alias = {}
    aliased = into is not None and into is not False
    if aliased:
        alias = {fixed + 1: 0}
        operands.append(into)
        specs.append(pl.BlockSpec(memory_space=pl.ANY))

    def call(z_ref, *refs):
        kernel(*refs[:fixed], *refs[fixed + aliased :])

    shape = (g, count, b, s) if into is False else (size, slots, b, s)
    out = pl.pallas_call(
        call,
        grid_spec=pltpu.PrefetchScalarGridSpec(
            num_scalar_prefetch=1,
            grid=(1, count // unit),
            in_specs=specs,
            out_specs=[pl.BlockSpec(block, own if into is False else at)]
            + [whole(v) for v in sums],
        ),
        out_shape=[jax.ShapeDtypeStruct(shape, bf16)]
        + [jax.ShapeDtypeStruct(v, f32) for v in sums],
        input_output_aliases=alias,
    )(line.reshape(1), *operands)
    return out if sums else out[0]


def scatter_sum(total):
    size = lax.axis_size("seq")
    bits = size.bit_length() - 1
    rows = total.shape[0] // size
    parts = total.reshape((2,) * bits + (rows, total.shape[1]))
    for bit in range(bits):
        axis = parts.ndim - 3
        own = (lax.axis_index("seq") >> bit) & 1
        keep = lax.dynamic_index_in_dim(parts, own, axis, keepdims=False)
        send = lax.dynamic_index_in_dim(parts, 1 - own, axis, keepdims=False)
        pairs = [(i, i ^ (1 << bit)) for i in range(size)]
        parts = keep + lax.ppermute(send, "seq", pairs)
    return parts


def channel_sum(value):
    size = lax.axis_size("ch")
    step = 1
    while step < size:
        value = value + lax.ppermute(value, "ch", [(i, i ^ step) for i in range(size)])
        step *= 2
    return value


def add_all(parts):
    return sum(parts[1:], parts[0])


def body(x, gate, og, f1, f2, tw):
    size = lax.axis_size("seq")
    g = size // LINE
    own_width, b, s = x.shape
    width = own_width * lax.axis_size("ch")
    blocks = f2.shape[0]
    slots = own_width // size
    by_peer = lambda v: v.reshape(size, slots, b, s)
    x, gate, og = by_peer(x), by_peer(gate), by_peer(og)
    count = slots // CHUNKS
    starts = [k * count for k in range(CHUNKS)]
    place = lax.axis_index("seq") // g
    lines = [place ^ k for k in range(LINE)]
    order = jnp.stack(lines)

    def reorder(m):
        m = m.reshape(LINE, -1, m.shape[1])[order].reshape(m.shape)
        return m.reshape(m.shape[0], LINE, -1)[:, order].reshape(m.shape)

    f2r = reorder(f2)
    f2rt = f2r.T
    groups = [[i * g + j for j in range(g)] for i in range(LINE)]

    def across(slabs):
        out = [slabs[0]] + [None] * (LINE - 1)
        for k in range(LINE - 1, 0, -1):
            out[k] = lax.ppermute(slabs[k], "seq", [(i, i ^ (k * g)) for i in range(size)])
        return out

    def within(slabs):
        return [
            lax.all_to_all(
                v.reshape(-1, b, s), "seq", 0, 0, axis_index_groups=groups, tiled=True
            ).reshape(v.shape)
            for v in slabs
        ]

    def grads_of(lo):
        return [stage(product_kernel, 8, z, lo, None, count, [gate, og], []) for z in lines]

    def firsts_of(lo):
        return [stage(first_kernel, 4, z, lo, None, count, [x], [f1, tw]) for z in lines]

    over = [across(grads_of(lo)) for lo in starts]
    vals_over = [across(firsts_of(lo)) for lo in starts]
    d_got, c_got, two_parts = [], [], []
    for c in range(CHUNKS):
        over[c] = within(over[c])
        made = mid_stage(mix_grad_kernel, over[c], f2rt)[0]
        d_got.append(across(within(made)))
    for c in range(CHUNKS):
        vals = within(vals_over[c])
        mixed, parts = mid_stage(mix_kernel, vals + over[c], f2r, [f2.shape])
        two_parts += parts
        c_got.append(across(within(mixed)))
    two_sum = reorder(add_all(two_parts))

    values_grad = gate_grad = None
    one_parts, tw_parts = [], []
    for lo, d in zip(starts, d_got):
        for z, slab in zip(lines, d):
            values_grad, one, tw_part = stage(
                last_kernel, 4, z, lo, slab, count, [x], [f1, tw], values_grad,
                [f1.shape, tw.shape],
            )
            one_parts.append(one)
            tw_parts.append(tw_part)
    rows = scatter_sum(jnp.concatenate([add_all(one_parts), two_sum], axis=1))
    sums = channel_sum(jnp.concatenate([rows, add_all(tw_parts)], axis=1))
    for lo, c in zip(starts, c_got):
        for z, slab in zip(lines, c):
            gate_grad = stage(product_kernel, 8, z, lo, slab, count, [og], [], gate_grad)
    one_rows = sums[:, :s]
    two_rows = sums[:, s : s + blocks]
    tw_rows = sums[:, s + blocks :]
    return (
        values_grad.reshape(own_width, b, s),
        gate_grad.reshape(own_width, b, s),
        one_rows * (1.0 / (width * blocks) ** 0.5),
        two_rows * (1.0 / (width * s) ** 0.5),
        tw_rows * (1.0 / width**0.5),
    )


def solution(mesh):
    return jax.shard_map(
        body,
        mesh=mesh,
        in_specs=(
            P("ch", "seq", None),
            P("ch", "seq", None),
            P("ch", "seq", None),
            P(),
            P(),
            P("seq", None),
        ),
        out_specs=(
            P("ch", "seq", None),
            P("ch", "seq", None),
            P("seq", None),
            P("seq", None),
            P("seq", None),
        ),
        check_vma=False,
    )
```

time: 2140 us -> 2010 us (0.939)
  the two profiles are of different devices: /device:TPU:0 before, /device:TPU:10 now
where the time goes in v2:
time: 2010 us; the launch traced here: 2000 us
  waiting for transfers between devices  1360 us (68%)
  starting transfers between devices  218 us (11%)
  Pallas kernels  199 us (10%)
  blocking collectives  192 us (10%)
  local copies, waits for them, and re-layouts  25.1 us (1%)
    ppermute x24, waiting for transfers between devices, across(): lax.ppermute(slabs[k], 'seq', [(i, i ^ k * g) for i in range(size)])  1000 us
    all_to_all x25, waiting for transfers between devices, within(): lax.all_to_all(v.reshape(-1, b, s), 'seq', 0, 0, axis_index_groups=groups...  203 us
    all_to_all x7, blocking collectives, within(): lax.all_to_all(v.reshape(-1, b, s), 'seq', 0, 0, axis_index_groups=groups...  192 us
    ppermute x4, waiting for transfers between devices, scatter_sum(): parts = keep + lax.ppermute(send, 'seq', pairs)  155 us
    pallas_call x32, Pallas kernels, stage(): pl.pallas_call(call, grid_spec=pltpu.PrefetchScalarGridSpec(num_scalar_pr...  151 us
    all_to_all x25, starting transfers between devices, within(): lax.all_to_all(v.reshape(-1, b, s), 'seq', 0, 0, axis_index_groups=groups...  115 us
    ppermute x24, starting transfers between devices, across(): lax.ppermute(slabs[k], 'seq', [(i, i ^ k * g) for i in range(size)])  97.6 us
    pallas_call x4, Pallas kernels, mid_stage(): pl.pallas_call(kernel, grid=(count // unit,), in_specs=[part] * len(slabs...  47.3 us
  transfers between devices with their start and end apart: 54, of which 33 were waited for; matrix products, arithmetic and copies ran while one was open for 1% of the time, Pallas kernels for 10%

profile of v2, /device:TPU:10, one launch (start us, length us, event | category | flops | bytes accessed | tf_op | source)
XLA Modules:
  0.0 2002.9 jit_solution(6151109535438729806)
XLA Ops:
  11.8 21.0 %all-to-all-done.8 = bf16[64,32,512]{2,1,0:T(8,128)(2,1)S(1)} async-done(((bf16[64,32,512]{2,1,0:T(8,128)(2,1)}), bf16[64,32,512]{2,1,0:T(8,128)(2,1)S(1)}, u32[]{:S(2)}, u32[]{:S(2)}) %all-to-all-start.8) | async-done | bytes 2097184 | tf_op jit(solution)/shard_map/all_to_all | solution.py:197
  43.1 19.0 all-to-all-done
  142.5 96.2 %collective-permute-done.7 = bf16[4,16,32,512]{3,2,1,0:T(8,128)(2,1)} collective-permute-done((bf16[4,16,32,512]{3,2,1,0:T(8,128)(2,1)}, bf16[4,16,32,512]{3,2,1,0:T(8,128)(2,1)}, u32[]{:S(2)}, u32[]{:S(2)}) %collective-permute-start.7) | collective-permute-done | bytes 2097184 | tf_op jit(solution)/shard_map/ppermute | solution.py:192
  251.3 122.2 %collective-permute-done.8 = bf16[4,16,32,512]{3,2,1,0:T(8,128)(2,1)} collective-permute-done((bf16[4,16,32,512]{3,2,1,0:T(8,128)(2,1)}, bf16[4,16,32,512]{3,2,1,0:T(8,128)(2,1)}, u32[]{:S(2)}, u32[]{:S(2)}) %collective-permute-start.8) | collective-permute-done | bytes 2097184 | tf_op jit(solution)/shard_map/ppermute | solution.py:192
  383.6 34.9 %collective-permute-done.1 = bf16[4,16,32,512]{3,2,1,0:T(8,128)(2,1)} collective-permute-done((bf16[4,16,32,512]{3,2,1,0:T(8,128)(2,1)}, bf16[4,16,32,512]{3,2,1,0:T(8,128)(2,1)}, u32[]{:S(2)}, u32[]{:S(2)}) %collective-permute-start.1) | collective-permute-done | bytes 2097184 | tf_op jit(solution)/shard_map/ppermute | solution.py:192
  428.5 32.8 %collective-permute-done.2 = bf16[4,16,32,512]{3,2,1,0:T(8,128)(2,1)} collective-permute-done((bf16[4,16,32,512]{3,2,1,0:T(8,128)(2,1)}, bf16[4,16,32,512]{3,2,1,0:T(8,128)(2,1)}, u32[]{:S(2)}, u32[]{:S(2)}) %collective-permute-start.2) | collective-permute-done | bytes 2097184 | tf_op jit(solution)/shard_map/ppermute | solution.py:192
  472.3 18.2 all-to-all-done.3
  499.5 34.4 %collective-permute-done.18 = bf16[4,16,32,512]{3,2,1,0:T(8,128)(2,1)} collective-permute-done((bf16[4,16,32,512]{3,2,1,0:T(8,128)(2,1)}, bf16[4,16,32,512]{3,2,1,0:T(8,128)(2,1)}, u32[]{:S(2)}, u32[]{:S(2)}) %collective-permute-start.18) | collective-permute-done | bytes 2097184 | tf_op jit(solution)/shard_map/ppermute | solution.py:192
  547.4 88.3 %collective-permute-done.19 = bf16[4,16,32,512]{3,2,1,0:T(8,128)(2,1)} collective-permute-done((bf16[4,16,32,512]{3,2,1,0:T(8,128)(2,1)}, bf16[4,16,32,512]{3,2,1,0:T(8,128)(2,1)}, u32[]{:S(2)}, u32[]{:S(2)}) %collective-permute-start.19) | collective-permute-done | bytes 2097184 | tf_op jit(solution)/shard_map/ppermute | solution.py:192
  649.1 32.6 %collective-permute-done.20 = bf16[4,16,32,512]{3,2,1,0:T(8,128)(2,1)} collective-permute-done((bf16[4,16,32,512]{3,2,1,0:T(8,128)(2,1)}, bf16[4,16,32,512]{3,2,1,0:T(8,128)(2,1)}, u32[]{:S(2)}, u32[]{:S(2)}) %collective-permute-start.20) | collective-permute-done | bytes 2097184 | tf_op jit(solution)/shard_map/ppermute | solution.py:192
  692.7 18.5 all-to-all-done.27
  720.2 106.5 %collective-permute-done.13 = bf16[4,16,32,512]{3,2,1,0:T(8,128)(2,1)} collective-permute-done((bf16[4,16,32,512]{3,2,1,0:T(8,128)(2,1)}, bf16[4,16,32,512]{3,2,1,0:T(8,128)(2,1)}, u32[]{:S(2)}, u32[]{:S(2)}) %collective-permute-start.13) | collective-permute-done | bytes 2097184 | tf_op jit(solution)/shard_map/ppermute | solution.py:192
  832.9 38.6 %collective-permute-done.14 = bf16[4,16,32,512]{3,2,1,0:T(8,128)(2,1)} collective-permute-done((bf16[4,16,32,512]{3,2,1,0:T(8,128)(2,1)}, bf16[4,16,32,512]{3,2,1,0:T(8,128)(2,1)}, u32[]{:S(2)}, u32[]{:S(2)}) %collective-permute-start.14) | collective-permute-done | bytes 2097184 | tf_op jit(solution)/shard_map/ppermute | solution.py:192
  900.0 29.1 %all_to_all.160 = bf16[64,32,512]{2,1,0:T(8,128)(2,1)} all-to-all(bf16[64,32,512]{2,1,0:T(8,128)(2,1)} %bitcast.203), channel_id=1, replica_groups={{0,2,4,6},{8,10,12,14},{16,18,20,22},{24,26,28,30},{1,3,5,7},{9,11,13,1..., dimensions={0} | all-to-all | bytes 4194304 | tf_op jit(solution)/shard_map/all_to_all | solution.py:197
  929.0 26.9 %all_to_all.161 = bf16[64,32,512]{2,1,0:T(8,128)(2,1)} all-to-all(bf16[64,32,512]{2,1,0:T(8,128)(2,1)S(1)} %bitcast.201), channel_id=1, replica_groups={{0,2,4,6},{8,10,12,14},{16,18,20,22},{24,26,28,30},{1,3,5,7},{9,11,13,1..., dimensions={0} | all-to-all | bytes 4194304 | tf_op jit(solution)/shard_map/all_to_all | solution.py:197
  955.9 25.3 %all_to_all.162 = bf16[64,32,512]{2,1,0:T(8,128)(2,1)} all-to-all(bf16[64,32,512]{2,1,0:T(8,128)(2,1)S(1)} %bitcast.199), channel_id=1, replica_groups={{0,2,4,6},{8,10,12,14},{16,18,20,22},{24,26,28,30},{1,3,5,7},{9,11,13,1..., dimensions={0} | all-to-all | bytes 4194304 | tf_op jit(solution)/shard_map/all_to_all | solution.py:197
  1005.5 29.1 %all_to_all.163 = bf16[64,32,512]{2,1,0:T(8,128)(2,1)} all-to-all(bf16[64,32,512]{2,1,0:T(8,128)(2,1)} %bitcast.202), channel_id=1, replica_groups={{0,2,4,6},{8,10,12,14},{16,18,20,22},{24,26,28,30},{1,3,5,7},{9,11,13,1..., dimensions={0} | all-to-all | bytes 4194304 | tf_op jit(solution)/shard_map/all_to_all | solution.py:197
  1034.6 27.0 %all_to_all.164 = bf16[64,32,512]{2,1,0:T(8,128)(2,1)} all-to-all(bf16[64,32,512]{2,1,0:T(8,128)(2,1)S(1)} %bitcast.200), channel_id=1, replica_groups={{0,2,4,6},{8,10,12,14},{16,18,20,22},{24,26,28,30},{1,3,5,7},{9,11,13,1..., dimensions={0} | all-to-all | bytes 4194304 | tf_op jit(solution)/shard_map/all_to_all | solution.py:197
  1061.6 25.3 %all_to_all.165 = bf16[64,32,512]{2,1,0:T(8,128)(2,1)} all-to-all(bf16[64,32,512]{2,1,0:T(8,128)(2,1)S(1)} %bitcast.198), channel_id=1, replica_groups={{0,2,4,6},{8,10,12,14},{16,18,20,22},{24,26,28,30},{1,3,5,7},{9,11,13,1..., dimensions={0} | all-to-all | bytes 4194304 | tf_op jit(solution)/shard_map/all_to_all | solution.py:197
  1111.2 28.8 %all_to_all.166 = bf16[64,32,512]{2,1,0:T(8,128)(2,1)} all-to-all(bf16[64,32,512]{2,1,0:T(8,128)(2,1)} %bitcast.197), channel_id=1, replica_groups={{0,2,4,6},{8,10,12,14},{16,18,20,22},{24,26,28,30},{1,3,5,7},{9,11,13,1..., dimensions={0} | all-to-all | bytes 4194304 | tf_op jit(solution)/shard_map/all_to_all | solution.py:197
  1145.5 22.5 %all-to-all-done.29 = bf16[64,32,512]{2,1,0:T(8,128)(2,1)} async-done(((bf16[64,32,512]{2,1,0:T(8,128)(2,1)}), bf16[64,32,512]{2,1,0:T(8,128)(2,1)}, u32[]{:S(2)}, u32[]{:S(2)}) %all-to-all-start.29) | async-done | bytes 2097184 | tf_op jit(solution)/shard_map/all_to_all | solution.py:197
  1254.3 84.2 %collective-permute-done.10.refs_0_ = bf16[4,16,32,512]{3,2,1,0:T(8,128)(2,1)} collective-permute-done((bf16[4,16,32,512]{3,2,1,0:T(8,128)(2,1)}, bf16[4,16,32,512]{3,2,1,0:T(8,128)(2,1)}, u32[]{:S(2)}, u32[]{:S(2)}) %collective-permute-start.10) | collective-permute-done | bytes 2097184 | tf_op jit(solution)/shard_map/ppermute | solution.py:192
  1345.8 128.5 %collective-permute-done.9.refs_0_ = bf16[4,16,32,512]{3,2,1,0:T(8,128)(2,1)} collective-permute-done((bf16[4,16,32,512]{3,2,1,0:T(8,128)(2,1)}, bf16[4,16,32,512]{3,2,1,0:T(8,128)(2,1)}, u32[]{:S(2)}, u32[]{:S(2)}) %collective-permute-start.9) | collective-permute-done | bytes 2097184 | tf_op jit(solution)/shard_map/ppermute | solution.py:192
  1496.1 21.8 %collective-permute-done.4.refs_0_ = bf16[4,16,32,512]{3,2,1,0:T(8,128)(2,1)} collective-permute-done((bf16[4,16,32,512]{3,2,1,0:T(8,128)(2,1)}, bf16[4,16,32,512]{3,2,1,0:T(8,128)(2,1)}, u32[]{:S(2)}, u32[]{:S(2)}) %collective-permute-start.4) | collective-permute-done | bytes 2097184 | tf_op jit(solution)/shard_map/ppermute | solution.py:192
  1525.2 38.7 %collective-permute-done.3.refs_0_ = bf16[4,16,32,512]{3,2,1,0:T(8,128)(2,1)} collective-permute-done((bf16[4,16,32,512]{3,2,1,0:T(8,128)(2,1)}, bf16[4,16,32,512]{3,2,1,0:T(8,128)(2,1)}, u32[]{:S(2)}, u32[]{:S(2)}) %collective-permute-start.3) | collective-permute-done | bytes 2097184 | tf_op jit(solution)/shard_map/ppermute | solution.py:192
  1583.2 19.9 collective-permute-done.24
  1607.0 18.4 all-to-all-done.20
  1646.7 127.0 %collective-permute-done.27 = f32[32,1024]{1,0:T(8,128)S(1)} collective-permute-done((f32[32,1024]{1,0:T(8,128)S(1)}, f32[32,1024]{1,0:T(8,128)S(1)}, u32[]{:S(2)}, u32[]{:S(2)}) %collective-permute-start.27) | collective-permute-done | bytes 131104 | tf_op jit(solution)/shard_map/ppermute | solution.py:149
  1773.7 68.9 %collective-permute-start.15 = (bf16[4,16,32,512]{3,2,1,0:T(8,128)(2,1)}, bf16[4,16,32,512]{3,2,1,0:T(8,128)(2,1)}, u32[]{:S(2)}, u32[]{:S(2)}) collective-permute-start(bf16[4,16,32,512]{3,2,1,0:T(8,128)(2,1)} %bitcast.57), channel_id=1, source_target_pairs={{0,24},{2,26},{4,28},{6,30},{8,16},{10,18},{12,20},{14,22},{16,8},... | collective-permute-start | bytes 6291464 | tf_op jit(solution)/shard_map/ppermute | solution.py:192
  1858.9 51.6 %collective-permute-done.21.refs_0_ = bf16[4,16,32,512]{3,2,1,0:T(8,128)(2,1)} collective-permute-done((bf16[4,16,32,512]{3,2,1,0:T(8,128)(2,1)}, bf16[4,16,32,512]{3,2,1,0:T(8,128)(2,1)}, u32[]{:S(2)}, u32[]{:S(2)}) %collective-permute-start.21) | collective-permute-done | bytes 2097184 | tf_op jit(solution)/shard_map/ppermute | solution.py:192
  1920.8 32.3 %collective-permute-done.16.refs_0_ = bf16[4,16,32,512]{3,2,1,0:T(8,128)(2,1)} collective-permute-done((bf16[4,16,32,512]{3,2,1,0:T(8,128)(2,1)}, bf16[4,16,32,512]{3,2,1,0:T(8,128)(2,1)}, u32[]{:S(2)}, u32[]{:S(2)}) %collective-permute-start.16) | collective-permute-done | bytes 2097184 | tf_op jit(solution)/shard_map/ppermute | solution.py:192
  1956.5 42.2 %collective-permute-done.15.refs_0_ = bf16[4,16,32,512]{3,2,1,0:T(8,128)(2,1)} collective-permute-done((bf16[4,16,32,512]{3,2,1,0:T(8,128)(2,1)}, bf16[4,16,32,512]{3,2,1,0:T(8,128)(2,1)}, u32[]{:S(2)}, u32[]{:S(2)}) %collective-permute-start.15) | collective-permute-done | bytes 2097184 | tf_op jit(solution)/shard_map/ppermute | solution.py:192
  (205 shorter events, 490.8 us)
Async XLA Ops:
  71.8 62.5 %collective-permute-start.6 = (bf16[4,16,32,512]{3,2,1,0:T(8,128)(2,1)}, bf16[4,16,32,512]{3,2,1,0:T(8,128)(2,1)}, u32[]{:S(2)}, u32[]{:S(2)}) collective-permute-start(bf16[4,16,32,512]{3,2,1,0:T(8,128)(2,1)} %shard_map.107), channel_id=1, source_target_pairs={{0,8},{2,10},{4,12},{6,14},{8,0},{10,2},{12,4},{14,6},{16,24},{18,... | collective-permute-start | bytes 6291464 | tf_op jit(solution)/shard_map/ppermute | solution.py:192
  99.9 138.8 %collective-permute-start.7 = (bf16[4,16,32,512]{3,2,1,0:T(8,128)(2,1)}, bf16[4,16,32,512]{3,2,1,0:T(8,128)(2,1)}, u32[]{:S(2)}, u32[]{:S(2)}) collective-permute-start(bf16[4,16,32,512]{3,2,1,0:T(8,128)(2,1)} %shard_map.108), channel_id=1, source_target_pairs={{0,16},{2,18},{4,20},{6,22},{8,24},{10,26},{12,28},{14,30},{16,0},... | collective-permute-start | bytes 6291464 | tf_op jit(solution)/shard_map/ppermute | solution.py:192
  134.4 104.4 %all-to-all-start.9 = ((bf16[64,32,512]{2,1,0:T(8,128)(2,1)}), bf16[64,32,512]{2,1,0:T(8,128)(2,1)S(1)}, u32[]{:S(2)}, u32[]{:S(2)}) async-start(bf16[64,32,512]{2,1,0:T(8,128)(2,1)} %bitcast.33), calls=%async_computation.9 | async-start | bytes 4194304 | tf_op jit(solution)/shard_map/all_to_all | solution.py:197
  142.0 231.6 %collective-permute-start.8 = (bf16[4,16,32,512]{3,2,1,0:T(8,128)(2,1)}, bf16[4,16,32,512]{3,2,1,0:T(8,128)(2,1)}, u32[]{:S(2)}, u32[]{:S(2)}) collective-permute-start(bf16[4,16,32,512]{3,2,1,0:T(8,128)(2,1)} %shard_map.109), channel_id=1, source_target_pairs={{0,24},{2,26},{4,28},{6,30},{8,16},{10,18},{12,20},{14,22},{16,8},... | collective-permute-start | bytes 6291464 | tf_op jit(solution)/shard_map/ppermute | solution.py:192
  240.0 133.5 %all-to-all-start.10 = ((bf16[64,32,512]{2,1,0:T(8,128)(2,1)}), bf16[64,32,512]{2,1,0:T(8,128)(2,1)}, u32[]{:S(2)}, u32[]{:S(2)}) async-start(bf16[64,32,512]{2,1,0:T(8,128)(2,1)} %bitcast.35), calls=%async_computation.10 | async-start | bytes 4194304 | tf_op jit(solution)/shard_map/all_to_all | solution.py:197
  247.9 170.5 %collective-permute-start.1 = (bf16[4,16,32,512]{3,2,1,0:T(8,128)(2,1)}, bf16[4,16,32,512]{3,2,1,0:T(8,128)(2,1)}, u32[]{:S(2)}, u32[]{:S(2)}) collective-permute-start(bf16[4,16,32,512]{3,2,1,0:T(8,128)(2,1)} %shard_map.103), channel_id=1, source_target_pairs={{0,16},{2,18},{4,20},{6,22},{8,24},{10,26},{12,28},{14,30},{16,0},... | collective-permute-start | bytes 6291464 | tf_op jit(solution)/shard_map/ppermute | solution.py:192
  381.1 80.2 %collective-permute-start.2 = (bf16[4,16,32,512]{3,2,1,0:T(8,128)(2,1)}, bf16[4,16,32,512]{3,2,1,0:T(8,128)(2,1)}, u32[]{:S(2)}, u32[]{:S(2)}) collective-permute-start(bf16[4,16,32,512]{3,2,1,0:T(8,128)(2,1)} %shard_map.104), channel_id=1, source_target_pairs={{0,24},{2,26},{4,28},{6,30},{8,16},{10,18},{12,20},{14,22},{16,8},... | collective-permute-start | bytes 6291464 | tf_op jit(solution)/shard_map/ppermute | solution.py:192
  472.2 61.7 %collective-permute-start.18 = (bf16[4,16,32,512]{3,2,1,0:T(8,128)(2,1)}, bf16[4,16,32,512]{3,2,1,0:T(8,128)(2,1)}, u32[]{:S(2)}, u32[]{:S(2)}) collective-permute-start(bf16[4,16,32,512]{3,2,1,0:T(8,128)(2,1)} %shard_map.125), channel_id=1, source_target_pairs={{0,8},{2,10},{4,12},{6,14},{8,0},{10,2},{12,4},{14,6},{16,24},{18,... | collective-permute-start | bytes 6291464 | tf_op jit(solution)/shard_map/ppermute | solution.py:192
  499.5 136.2 %collective-permute-start.19 = (bf16[4,16,32,512]{3,2,1,0:T(8,128)(2,1)}, bf16[4,16,32,512]{3,2,1,0:T(8,128)(2,1)}, u32[]{:S(2)}, u32[]{:S(2)}) collective-permute-start(bf16[4,16,32,512]{3,2,1,0:T(8,128)(2,1)} %shard_map.126), channel_id=1, source_target_pairs={{0,16},{2,18},{4,20},{6,22},{8,24},{10,26},{12,28},{14,30},{16,0},... | collective-permute-start | bytes 6291464 | tf_op jit(solution)/shard_map/ppermute | solution.py:192
  535.3 100.5 %all-to-all-start.25 = ((bf16[64,32,512]{2,1,0:T(8,128)(2,1)}), bf16[64,32,512]{2,1,0:T(8,128)(2,1)}, u32[]{:S(2)}, u32[]{:S(2)}) async-start(bf16[64,32,512]{2,1,0:T(8,128)(2,1)} %bitcast.66), calls=%async_computation.25 | async-start | bytes 4194304 | tf_op jit(solution)/shard_map/all_to_all | solution.py:197
  544.9 136.8 %collective-permute-start.20 = (bf16[4,16,32,512]{3,2,1,0:T(8,128)(2,1)}, bf16[4,16,32,512]{3,2,1,0:T(8,128)(2,1)}, u32[]{:S(2)}, u32[]{:S(2)}) collective-permute-start(bf16[4,16,32,512]{3,2,1,0:T(8,128)(2,1)} %shard_map.127), channel_id=1, source_target_pairs={{0,24},{2,26},{4,28},{6,30},{8,16},{10,18},{12,20},{14,22},{16,8},... | collective-permute-start | bytes 6291464 | tf_op jit(solution)/shard_map/ppermute | solution.py:192
  692.7 134.1 %collective-permute-start.13 = (bf16[4,16,32,512]{3,2,1,0:T(8,128)(2,1)}, bf16[4,16,32,512]{3,2,1,0:T(8,128)(2,1)}, u32[]{:S(2)}, u32[]{:S(2)}) collective-permute-start(bf16[4,16,32,512]{3,2,1,0:T(8,128)(2,1)} %shard_map.121), channel_id=1, source_target_pairs={{0,16},{2,18},{4,20},{6,22},{8,24},{10,26},{12,28},{14,30},{16,0},... | collective-permute-start | bytes 6291464 | tf_op jit(solution)/shard_map/ppermute | solution.py:192
  711.2 115.6 %all-to-all-start.17 = ((bf16[64,32,512]{2,1,0:T(8,128)(2,1)}), bf16[64,32,512]{2,1,0:T(8,128)(2,1)S(1)}, u32[]{:S(2)}, u32[]{:S(2)}) async-start(bf16[64,32,512]{2,1,0:T(8,128)(2,1)} %bitcast.50), calls=%async_computation.17 | async-start | bytes 4194304 | tf_op jit(solution)/shard_map/all_to_all | solution.py:197
  720.2 151.2 %collective-permute-start.14 = (bf16[4,16,32,512]{3,2,1,0:T(8,128)(2,1)}, bf16[4,16,32,512]{3,2,1,0:T(8,128)(2,1)}, u32[]{:S(2)}, u32[]{:S(2)}) collective-permute-start(bf16[4,16,32,512]{3,2,1,0:T(8,128)(2,1)} %shard_map.122), channel_id=1, source_target_pairs={{0,24},{2,26},{4,28},{6,30},{8,16},{10,18},{12,20},{14,22},{16,8},... | collective-permute-start | bytes 6291464 | tf_op jit(solution)/shard_map/ppermute | solution.py:192
  1145.5 62.7 %collective-permute-start.11 = (bf16[4,16,32,512]{3,2,1,0:T(8,128)(2,1)}, bf16[4,16,32,512]{3,2,1,0:T(8,128)(2,1)S(1)}, u32[]{:S(2)}, u32[]{:S(2)}) collective-permute-start(bf16[4,16,32,512]{3,2,1,0:T(8,128)(2,1)} %bitcast.191), channel_id=1, source_target_pairs={{0,8},{2,10},{4,12},{6,14},{8,0},{10,2},{12,4},{14,6},{16,24},{18,... | collective-permute-start | bytes 6291464 | tf_op jit(solution)/shard_map/ppermute | solution.py:192
  1201.9 136.7 %collective-permute-start.10 = (bf16[4,16,32,512]{3,2,1,0:T(8,128)(2,1)}, bf16[4,16,32,512]{3,2,1,0:T(8,128)(2,1)}, u32[]{:S(2)}, u32[]{:S(2)}) collective-permute-start(bf16[4,16,32,512]{3,2,1,0:T(8,128)(2,1)} %bitcast.189), channel_id=1, source_target_pairs={{0,16},{2,18},{4,20},{6,22},{8,24},{10,26},{12,28},{14,30},{16,0},... | collective-permute-start | bytes 6291464 | tf_op jit(solution)/shard_map/ppermute | solution.py:192
  1201.9 272.4 %collective-permute-start.9 = (bf16[4,16,32,512]{3,2,1,0:T(8,128)(2,1)}, bf16[4,16,32,512]{3,2,1,0:T(8,128)(2,1)}, u32[]{:S(2)}, u32[]{:S(2)}) collective-permute-start(bf16[4,16,32,512]{3,2,1,0:T(8,128)(2,1)} %bitcast.187), channel_id=1, source_target_pairs={{0,24},{2,26},{4,28},{6,30},{8,16},{10,18},{12,20},{14,22},{16,8},... | collective-permute-start | bytes 6291464 | tf_op jit(solution)/shard_map/ppermute | solution.py:192
  1204.4 284.5 %collective-permute-start.5 = (bf16[4,16,32,512]{3,2,1,0:T(8,128)(2,1)}, bf16[4,16,32,512]{3,2,1,0:T(8,128)(2,1)}, u32[]{:S(2)}, u32[]{:S(2)}) collective-permute-start(bf16[4,16,32,512]{3,2,1,0:T(8,128)(2,1)} %bitcast.188), channel_id=1, source_target_pairs={{0,8},{2,10},{4,12},{6,14},{8,0},{10,2},{12,4},{14,6},{16,24},{18,... | collective-permute-start | bytes 6291464 | tf_op jit(solution)/shard_map/ppermute | solution.py:192
  1206.3 311.6 %collective-permute-start.4 = (bf16[4,16,32,512]{3,2,1,0:T(8,128)(2,1)}, bf16[4,16,32,512]{3,2,1,0:T(8,128)(2,1)}, u32[]{:S(2)}, u32[]{:S(2)}) collective-permute-start(bf16[4,16,32,512]{3,2,1,0:T(8,128)(2,1)} %bitcast.186), channel_id=1, source_target_pairs={{0,16},{2,18},{4,20},{6,22},{8,24},{10,26},{12,28},{14,30},{16,0},... | collective-permute-start | bytes 6291464 | tf_op jit(solution)/shard_map/ppermute | solution.py:192
  1208.2 355.7 %collective-permute-start.3 = (bf16[4,16,32,512]{3,2,1,0:T(8,128)(2,1)}, bf16[4,16,32,512]{3,2,1,0:T(8,128)(2,1)}, u32[]{:S(2)}, u32[]{:S(2)}) collective-permute-start(bf16[4,16,32,512]{3,2,1,0:T(8,128)(2,1)} %bitcast.185), channel_id=1, source_target_pairs={{0,24},{2,26},{4,28},{6,30},{8,16},{10,18},{12,20},{14,22},{16,8},... | collective-permute-start | bytes 6291464 | tf_op jit(solution)/shard_map/ppermute | solution.py:192
  1225.8 351.3 %all-to-all-start.21 = ((bf16[64,32,512]{2,1,0:T(8,128)(2,1)}), bf16[64,32,512]{2,1,0:T(8,128)(2,1)}, u32[]{:S(2)}, u32[]{:S(2)}) async-start(bf16[64,32,512]{2,1,0:T(8,128)(2,1)} %bitcast.190), calls=%async_computation.21 | async-start | bytes 4194304 | tf_op jit(solution)/shard_map/all_to_all | solution.py:197
  1577.1 48.3 %all-to-all-start.20 = ((bf16[64,32,512]{2,1,0:T(8,128)(2,1)}), bf16[64,32,512]{2,1,0:T(8,128)(2,1)}, u32[]{:S(2)}, u32[]{:S(2)}) async-start(bf16[64,32,512]{2,1,0:T(8,128)(2,1)} %bitcast.184), calls=%async_computation.20 | async-start | bytes 4194304 | tf_op jit(solution)/shard_map/all_to_all | solution.py:197
  1583.2 61.6 %collective-permute-start.23 = (bf16[4,16,32,512]{3,2,1,0:T(8,128)(2,1)}, bf16[4,16,32,512]{3,2,1,0:T(8,128)(2,1)}, u32[]{:S(2)}, u32[]{:S(2)}) collective-permute-start(bf16[4,16,32,512]{3,2,1,0:T(8,128)(2,1)} %bitcast.183), channel_id=1, source_target_pairs={{0,8},{2,10},{4,12},{6,14},{8,0},{10,2},{12,4},{14,6},{16,24},{18,... | collective-permute-start | bytes 6291464 | tf_op jit(solution)/shard_map/ppermute | solution.py:192
  1625.4 217.2 %all-to-all-start.31 = ((bf16[64,32,512]{2,1,0:T(8,128)(2,1)}), bf16[64,32,512]{2,1,0:T(8,128)(2,1)S(1)}, u32[]{:S(2)}, u32[]{:S(2)}) async-start(bf16[64,32,512]{2,1,0:T(8,128)(2,1)} %bitcast.182), calls=%async_computation.31 | async-start | bytes 4194304 | tf_op jit(solution)/shard_map/all_to_all | solution.py:197
  1630.5 218.1 %collective-permute-start.22 = (bf16[4,16,32,512]{3,2,1,0:T(8,128)(2,1)}, bf16[4,16,32,512]{3,2,1,0:T(8,128)(2,1)}, u32[]{:S(2)}, u32[]{:S(2)}) collective-permute-start(bf16[4,16,32,512]{3,2,1,0:T(8,128)(2,1)} %bitcast.75), channel_id=1, source_target_pairs={{0,16},{2,18},{4,20},{6,22},{8,24},{10,26},{12,28},{14,30},{16,0},... | collective-permute-start | bytes 6291464 | tf_op jit(solution)/shard_map/ppermute | solution.py:192
  1639.7 134.0 %collective-permute-start.27 = (f32[32,1024]{1,0:T(8,128)S(1)}, f32[32,1024]{1,0:T(8,128)S(1)}, u32[]{:S(2)}, u32[]{:S(2)}) collective-permute-start(f32[32,1024]{1,0:T(8,128)S(1)} %dynamic-slice_bitcast_fusion.2), channel_id=1, source_target_pairs={{0,16},{2,18},{4,20},{6,22},{8,24},{10,26},{12,28},{14,30},{16,0},... | collective-permute-start | bytes 393224 | tf_op jit(solution)/shard_map/ppermute | solution.py:149
  1643.2 267.3 %collective-permute-start.21 = (bf16[4,16,32,512]{3,2,1,0:T(8,128)(2,1)}, bf16[4,16,32,512]{3,2,1,0:T(8,128)(2,1)}, u32[]{:S(2)}, u32[]{:S(2)}) collective-permute-start(bf16[4,16,32,512]{3,2,1,0:T(8,128)(2,1)} %bitcast.73), channel_id=1, source_target_pairs={{0,24},{2,26},{4,28},{6,30},{8,16},{10,18},{12,20},{14,22},{16,8},... | collective-permute-start | bytes 6291464 | tf_op jit(solution)/shard_map/ppermute | solution.py:192
  1643.2 274.1 %collective-permute-start.17 = (bf16[4,16,32,512]{3,2,1,0:T(8,128)(2,1)}, bf16[4,16,32,512]{3,2,1,0:T(8,128)(2,1)}, u32[]{:S(2)}, u32[]{:S(2)}) collective-permute-start(bf16[4,16,32,512]{3,2,1,0:T(8,128)(2,1)} %bitcast.61), channel_id=1, source_target_pairs={{0,8},{2,10},{4,12},{6,14},{8,0},{10,2},{12,4},{14,6},{16,24},{18,... | collective-permute-start | bytes 6291464 | tf_op jit(solution)/shard_map/ppermute | solution.py:192
  1644.8 308.4 %collective-permute-start.16 = (bf16[4,16,32,512]{3,2,1,0:T(8,128)(2,1)}, bf16[4,16,32,512]{3,2,1,0:T(8,128)(2,1)}, u32[]{:S(2)}, u32[]{:S(2)}) collective-permute-start(bf16[4,16,32,512]{3,2,1,0:T(8,128)(2,1)} %bitcast.59), channel_id=1, source_target_pairs={{0,16},{2,18},{4,20},{6,22},{8,24},{10,26},{12,28},{14,30},{16,0},... | collective-permute-start | bytes 6291464 | tf_op jit(solution)/shard_map/ppermute | solution.py:192
  1773.7 225.0 %collective-permute-start.15 = (bf16[4,16,32,512]{3,2,1,0:T(8,128)(2,1)}, bf16[4,16,32,512]{3,2,1,0:T(8,128)(2,1)}, u32[]{:S(2)}, u32[]{:S(2)}) collective-permute-start(bf16[4,16,32,512]{3,2,1,0:T(8,128)(2,1)} %bitcast.57), channel_id=1, source_target_pairs={{0,24},{2,26},{4,28},{6,30},{8,16},{10,18},{12,20},{14,22},{16,8},... | collective-permute-start | bytes 6291464 | tf_op jit(solution)/shard_map/ppermute | solution.py:192
  1843.9 70.0 %all-to-all-start.23 = ((bf16[64,32,512]{2,1,0:T(8,128)(2,1)}), bf16[64,32,512]{2,1,0:T(8,128)(2,1)}, u32[]{:S(2)}, u32[]{:S(2)}) async-start(bf16[64,32,512]{2,1,0:T(8,128)(2,1)} %bitcast.181), calls=%async_computation.23 | async-start | bytes 4194304 | tf_op jit(solution)/shard_map/all_to_all | solution.py:197
  1848.6 153.6 %collective-permute-start.28 = (f32[32,1536]{1,0:T(8,128)S(1)}, f32[32,1536]{1,0:T(8,128)S(1)}, u32[]{:S(2)}, u32[]{:S(2)}) collective-permute-start(f32[32,1536]{1,0:T(8,128)S(1)} %pad_maximum_fusion), channel_id=1, source_target_pairs={{0,1},{1,0},{2,3},{3,2},{4,5},{5,4},{6,7},{7,6},{8,9},{9,8},{10,11... | collective-permute-start | bytes 589832 | tf_op jit(solution)/shard_map/ppermute | solution.py:157
  (51 other events, 1873.7 us)
